TPU v7x, 32 devices: a whole 2x2x4 slice. The times are simulated.
32 devices in a mesh: tm: 8 (over z, x), space: 4 (over y, core).
Axes of the slice: x: 2, y: 2, z: 4, core: 2. Of those that a mesh axis runs over, the one named last changes fastest.
Arguments:
- guess: float32 [8, 5, 2, 32, 64, 128], P('tm', None, None, 'space'), may hold values from 0 to 1
- feed_rate: float32 [32, 64, 128], P('space'), may hold values from 0.05 to 0.5
- kill_rate: float32 [32, 64, 128], P('space'), may hold values from 0.05 to 0.5
Outputs:
- end_state: float32 [8, 2, 32, 64, 128], P('tm', None, 'space')
- next_nodes: float32 [8, 5, 2, 32, 64, 128], P('tm', None, None, 'space')
All inputs are finite; a program needn't handle non-finite values.
Results may differ from a plain program's by a relative error of at most 0.00002.
Values sent between devices are 32-bit elements; how exact they have to be, the bound alone decides.
A program may use at most 64 MiB of HBM per device.

v0:
```python
import math

import jax
import jax.numpy as jnp
import numpy as np
from jax import lax
from jax.sharding import PartitionSpec as P

SWEEPS = 4


substrate_spread = 0.2
catalyst_spread = 0.1
slab_time = 0.5


def padded_2(cells, sides, width):
    for axis, dim in sides:
        count = lax.axis_size(axis)
        head = lax.slice_in_dim(cells, 0, width, axis=dim)
        tail = lax.slice_in_dim(cells, cells.shape[dim] - width, cells.shape[dim], axis=dim)
        cells = jnp.concatenate(
            [
                lax.ppermute(tail, axis, [(i, (i + 1) % count) for i in range(count)]),
                cells,
                lax.ppermute(head, axis, [((i + 1) % count, i) for i in range(count)]),
            ],
            axis=dim,
        )
    return cells


def passed_along(block, axis, distance):
    devices = range(lax.axis_size(axis))
    route = [(i - distance, i) for i in devices if i - distance in devices]
    return lax.ppermute(block, axis, route)


def from_root(x, axis, root):
    mine = lax.axis_index(axis) == root
    return lax.psum(jnp.where(mine, x, jnp.zeros_like(x)), axis)


def lobatto_table():
    spread_root = math.sqrt(3.0 / 7.0)
    node_times = [0.0, (1.0 - spread_root) / 2.0, 0.5, (1.0 + spread_root) / 2.0, 1.0]
    table = [[0.0] * 5 for blank in range(5)]
    for column in range(5):
        coeffs = [1.0]
        divisor = 1.0
        for other_node in range(5):
            if other_node != column:
                product = [0.0] * (len(coeffs) + 1)
                for power, entry in enumerate(coeffs):
                    product[power + 1] += entry
                    product[power] -= node_times[other_node] * entry
                coeffs = product
                divisor *= node_times[column] - node_times[other_node]
        for row_index in range(5):
            upper = node_times[row_index]
            total_sum = 0.0
            for power, entry in enumerate(coeffs):
                total_sum += entry / (power + 1) * upper ** (power + 1)
            table[row_index][column] = total_sum / divisor
    return (np.array(node_times), np.array(table))


def reaction_rates(fields, laplace_terms, feed_rate, kill_rate):
    substrate = fields[..., 0, :, :, :]
    catalyst = fields[..., 1, :, :, :]
    reacting = substrate * catalyst * catalyst
    grow_sub = (
        substrate_spread * laplace_terms[..., 0, :, :, :] - reacting + feed_rate * (1.0 - substrate)
    )
    grow_cat = (
        catalyst_spread * laplace_terms[..., 1, :, :, :]
        + reacting
        - (feed_rate + kill_rate) * catalyst
    )
    return jnp.stack([grow_sub, grow_cat], axis=-4)


def padded_rates(padded, feed_rate, kill_rate):
    center = padded[..., 1:-1, :, :]
    total = -6.0 * center + padded[..., 2:, :, :] + padded[..., :-2, :, :]
    for axis_id in (-2, -1):
        total = total + jnp.roll(center, 1, axis_id) + jnp.roll(center, -1, axis_id)
    return reaction_rates(center, total, feed_rate, kill_rate)


def combine(start_pair, rates_all, weights):
    increment = jnp.zeros_like(rates_all)
    for column in range(weights.shape[1]):
        scale_col = jnp.asarray(weights[:, column], jnp.float32).reshape((-1, 1, 1, 1, 1))
        increment = increment + scale_col * rates_all[column][None]
    return start_pair[None] + slab_time * increment


def shards(guess, feed_rate, kill_rate):
    node_times, weights = lobatto_table()
    node_fields = guess[0]
    first_start = guess[0, 0]
    is_first = lax.axis_index("tm") == 0
    for sweep_index in range(SWEEPS):
        padded = padded_2(node_fields, (("space", 2),), 1)
        rates_all = padded_rates(padded, feed_rate, kill_rate)
        moved = passed_along(node_fields[-1], "tm", 1)
        start_pair = jnp.where(is_first, first_start, moved)
        node_fields = combine(start_pair, rates_all, weights)
    end_pair = node_fields[-1]
    root_index = lax.axis_size("tm") - 1
    last_pair = from_root(end_pair, "tm", root_index)
    padded_last = padded_2(last_pair, (("space", 1),), 1)
    seed_rate = padded_rates(padded_last, feed_rate, kill_rate)
    offsets = jnp.asarray(node_times, jnp.float32).reshape((-1, 1, 1, 1, 1))
    next_one = last_pair[None] + slab_time * offsets * seed_rate[None]
    return (end_pair[None], next_one[None])


def solution(mesh):
    placed = (
        P("tm", None, None, "space", None, None),
        P("space", None, None),
        P("space", None, None),
    )
    return jax.shard_map(
        shards,
        mesh=mesh,
        in_specs=placed,
        out_specs=(P("tm", None, "space", None, None), P("tm", None, None, "space", None, None)),
        check_vma=False,
    )
```

profile of v0, /device:TPU:0, one launch (start us, length us, event | category | flops | bytes accessed | tf_op | source)
XLA Modules:
  0.0 203.1 jit_solution(5632370206099398381)
XLA Ops:
  7.2 1.9 fusion.115
  9.1 2.4 %collective-permute-start.1 = (f32[5,2,1,64,128]{4,3,2,1,0:T(8,128)}, f32[5,2,1,64,128]{4,3,2,1,0:T(8,128)}, u32[]{:S(2)}, u32[]{:S(2)}) collective-permute-start(f32[5,2,1,64,128]{4,3,2,1,0:T(8,128)} %get-tuple-element.70), channel_id=1, source_target_pairs={{1,0},{2,1},{3,2},{0,3},{5,4},{6,5},{7,6},{4,7},{9,8},{10,9},{11,1... | collective-permute-start | bytes 983048 | tf_op jit(solution)/shard_map/ppermute | solution.py:26
  11.5 1.9 slice_bitcast_fusion.3
  13.4 4.5 %collective-permute-start = (f32[2,8,64,128]{3,2,1,0:T(8,128)}, f32[2,8,64,128]{3,2,1,0:T(8,128)}, u32[]{:S(2)}, u32[]{:S(2)}) collective-permute-start(f32[2,8,64,128]{3,2,1,0:T(8,128)} %slice_bitcast_fusion.3), channel_id=1, source_target_pairs={{0,4},{4,8},{8,12},{12,16},{16,20},{20,24},{24,28},{1,5},{5,9},{9,... | collective-permute-start | bytes 1572872 | tf_op jit(solution)/shard_map/ppermute | solution.py:36
  17.9 5.8 %fusion.111 = (f32[5,2,8,64,127]{4,3,2,1,0:T(8,128)}, f32[5,2,8,64,127]{4,3,2,1,0:T(8,128)}) fusion(f32[5,2,8,64,128]{4,3,2,1,0:T(8,128)} %bitcast.97), kind=kLoop, calls=%fused_computation.190 | loop fusion | bytes 10403840 | tf_op jit(solution)/shard_map/jit(_roll_static)/slice | solution.py:87
  23.6 3.4 %fusion.112 = (f32[5,2,8,64,1]{4,3,2,1,0:T(8,128)}, f32[5,2,8,64,1]{4,3,2,1,0:T(8,128)}) fusion(f32[5,2,8,64,128]{4,3,2,1,0:T(8,128)S(1)} %bitcast.98), kind=kLoop, calls=%fused_computation.191 | loop fusion | bytes 81920 | tf_op jit(solution)/shard_map/jit(_roll_static)/slice | solution.py:87
  27.1 3.0 %fusion.113 = (f32[5,2,8,63,128]{4,3,2,1,0:T(8,128)}, f32[5,2,8,63,128]{4,3,2,1,0:T(8,128)}) fusion(f32[5,2,8,64,128]{4,3,2,1,0:T(8,128)S(1)} %bitcast.99), kind=kLoop, calls=%fused_computation.192 | loop fusion | bytes 10321920 | tf_op jit(solution)/shard_map/jit(_roll_static)/slice | solution.py:87
  32.9 7.0 %fusion.22 = f32[5,2,8,64,128]{4,3,2,1,0:T(8,128)S(1)} fusion(f32[5,2,8,64,128]{4,3,2,1,0:T(8,128)S(1)} %bitcast.101, f32[5,2,1,64,128]{4,3,2,1,0:T(8,128)} %collective-permute-done.2, f32[5,2,1,64,128]{4,3,2,1,0:T(8,128)} %collective-permute-done.1, f32[5,2,8,63,128]{4,3,2,1,0:T(8,128)} %get-tuple-element.67, ...), kind=kLoop, calls=%fused_computation.61 | loop fusion | flops 8519680 | bytes 16384000 | tf_op jit(solution)/shard_map/add | solution.py:87
  46.9 4.2 %collective-permute-start.3 = (f32[2,8,64,128]{3,2,1,0:T(8,128)S(1)}, f32[2,8,64,128]{3,2,1,0:T(8,128)}, u32[]{:S(2)}, u32[]{:S(2)}) collective-permute-start(f32[2,8,64,128]{3,2,1,0:T(8,128)S(1)} %slice_bitcast_fusion.2), channel_id=1, source_target_pairs={{0,4},{4,8},{8,12},{12,16},{16,20},{20,24},{24,28},{1,5},{5,9},{9,... | collective-permute-start | bytes 1572872 | tf_op jit(solution)/shard_map/ppermute | solution.py:36
  51.2 3.8 %collective-permute-done.4 = f32[5,2,1,64,128]{4,3,2,1,0:T(8,128)S(1)} collective-permute-done((f32[5,2,1,64,128]{4,3,2,1,0:T(8,128)S(1)}, f32[5,2,1,64,128]{4,3,2,1,0:T(8,128)S(1)}, u32[]{:S(2)}, u32[]{:S(2)}) %collective-permute-start.4) | collective-permute-done | bytes 327712 | tf_op jit(solution)/shard_map/ppermute | solution.py:26
  56.0 2.9 %fusion.16 = f32[5,2,8,64,128]{4,3,2,1,0:T(8,128)S(1)} fusion(f32[5,2,8,64,128]{4,3,2,1,0:T(8,128)S(1)} %multiply_add_fusion.3, f32[5,2,1,64,128]{4,3,2,1,0:T(8,128)S(1)} %collective-permute-done.5, f32[5,2,1,64,128]{4,3,2,1,0:T(8,128)S(1)} %collective-permute-done.4, f32[5,2,8,63,128]{4,3,2,1,0:T(8,128)S(1)} %get-tuple-element.52, ...), kind=kLoop, calls=%fused_computation.53 | loop fusion | flops 8519680 | bytes 16384000 | tf_op jit(solution)/shard_map/add | solution.py:87
  60.2 2.2 %collective-permute-done.3 = f32[2,8,64,128]{3,2,1,0:T(8,128)} collective-permute-done((f32[2,8,64,128]{3,2,1,0:T(8,128)S(1)}, f32[2,8,64,128]{3,2,1,0:T(8,128)}, u32[]{:S(2)}, u32[]{:S(2)}) %collective-permute-start.3) | collective-permute-done | bytes 524320 | tf_op jit(solution)/shard_map/ppermute | solution.py:36
  67.1 6.3 %collective-permute-start.6 = (f32[2,8,64,128]{3,2,1,0:T(8,128)S(1)}, f32[2,8,64,128]{3,2,1,0:T(8,128)}, u32[]{:S(2)}, u32[]{:S(2)}) collective-permute-start(f32[2,8,64,128]{3,2,1,0:T(8,128)S(1)} %slice_bitcast_fusion.1), channel_id=1, source_target_pairs={{0,4},{4,8},{8,12},{12,16},{16,20},{20,24},{24,28},{1,5},{5,9},{9,... | collective-permute-start | bytes 1572872 | tf_op jit(solution)/shard_map/ppermute | solution.py:36
  74.8 1.6 collective-permute-done.8
  76.5 2.9 %fusion.10 = f32[5,2,8,64,128]{4,3,2,1,0:T(8,128)S(1)} fusion(f32[5,2,8,64,128]{4,3,2,1,0:T(8,128)S(1)} %multiply_add_fusion.2, f32[5,2,1,64,128]{4,3,2,1,0:T(8,128)S(1)} %collective-permute-done.8, f32[5,2,1,64,128]{4,3,2,1,0:T(8,128)S(1)} %collective-permute-done.7, f32[5,2,8,63,128]{4,3,2,1,0:T(8,128)S(1)} %get-tuple-element.37, ...), kind=kLoop, calls=%fused_computation.45 | loop fusion | flops 8519680 | bytes 16384000 | tf_op jit(solution)/shard_map/add | solution.py:87
  80.7 4.1 %collective-permute-done.6 = f32[2,8,64,128]{3,2,1,0:T(8,128)} collective-permute-done((f32[2,8,64,128]{3,2,1,0:T(8,128)S(1)}, f32[2,8,64,128]{3,2,1,0:T(8,128)}, u32[]{:S(2)}, u32[]{:S(2)}) %collective-permute-start.6) | collective-permute-done | bytes 524320 | tf_op jit(solution)/shard_map/ppermute | solution.py:36
  90.5 5.8 %collective-permute-start.9 = (f32[2,8,64,128]{3,2,1,0:T(8,128)}, f32[2,8,64,128]{3,2,1,0:T(8,128)S(1)}, u32[]{:S(2)}, u32[]{:S(2)}) collective-permute-start(f32[2,8,64,128]{3,2,1,0:T(8,128)} %slice_bitcast_fusion), channel_id=1, source_target_pairs={{0,4},{4,8},{8,12},{12,16},{16,20},{20,24},{24,28},{1,5},{5,9},{9,... | collective-permute-start | bytes 1572872 | tf_op jit(solution)/shard_map/ppermute | solution.py:36
  97.2 2.2 %collective-permute-done.11 = f32[5,2,1,64,128]{4,3,2,1,0:T(8,128)S(1)} collective-permute-done((f32[5,2,1,64,128]{4,3,2,1,0:T(8,128)S(1)}, f32[5,2,1,64,128]{4,3,2,1,0:T(8,128)S(1)}, u32[]{:S(2)}, u32[]{:S(2)}) %collective-permute-start.11) | collective-permute-done | bytes 327712 | tf_op jit(solution)/shard_map/ppermute | solution.py:24
  99.4 2.9 %fusion.4 = f32[5,2,8,64,128]{4,3,2,1,0:T(8,128)S(1)} fusion(f32[5,2,8,64,128]{4,3,2,1,0:T(8,128)S(1)} %multiply_add_fusion.1, f32[5,2,1,64,128]{4,3,2,1,0:T(8,128)S(1)} %collective-permute-done.11, f32[5,2,1,64,128]{4,3,2,1,0:T(8,128)S(1)} %collective-permute-done.10, f32[5,2,8,63,128]{4,3,2,1,0:T(8,128)S(1)} %get-tuple-element.22, ...), kind=kLoop, calls=%fused_computation.37 | loop fusion | flops 8519680 | bytes 16384000 | tf_op jit(solution)/shard_map/add | solution.py:87
  104.3 4.2 %collective-permute-done.9 = f32[2,8,64,128]{3,2,1,0:T(8,128)S(1)} collective-permute-done((f32[2,8,64,128]{3,2,1,0:T(8,128)}, f32[2,8,64,128]{3,2,1,0:T(8,128)S(1)}, u32[]{:S(2)}, u32[]{:S(2)}) %collective-permute-start.9) | collective-permute-done | bytes 524320 | tf_op jit(solution)/shard_map/ppermute | solution.py:36
  108.6 3.1 %select_bitcast_fusion = (f32[2,8,64,128]{3,2,1,0:T(8,128)}, f32[1,2,8,64,128]{4,3,2,1,0:T(8,128)}) fusion(pred[]{:T(512)S(6)} %eq.7, f32[2,8,64,128]{3,2,1,0:T(8,128)S(1)} %get-tuple-element.15, f32[1]{0:T(128)} %slice.546, f32[2,8,64,128]{3,2,1,0:T(8,128)S(1)} %get-tuple-element.16, f32[1]{0:T(128)} %slice.545, ...), kind=kLoop, calls=%fused_computation.160 | loop fusion | flops 1310720 | bytes 4194317 | tf_op jit(solution)/shard_map/jit(_where)/select_n | solution.py:41
  111.7 76.1 %all-reduce.2.cloned.1.call-done = f32[2,8,64,128]{3,2,1,0:T(8,128)} async-done(((f32[2,8,64,128]{3,2,1,0:T(8,128)}), f32[2,8,64,128]{3,2,1,0:T(8,128)}) %all-reduce.2.cloned.1.call-update) | async-done | bytes 524304 | tf_op jit(solution)/shard_map/psum | solution.py:41
  191.0 2.2 %collective-permute-done.13 = f32[2,1,64,128]{3,2,1,0:T(8,128)S(1)} collective-permute-done((f32[2,1,64,128]{3,2,1,0:T(8,128)S(1)}, f32[2,1,64,128]{3,2,1,0:T(8,128)S(1)}, u32[]{:S(2)}, u32[]{:S(2)}) %collective-permute-start.13) | collective-permute-done | bytes 65568 | tf_op jit(solution)/shard_map/ppermute | solution.py:24
  194.3 1.9 multiply_add_fusion
  (83 shorter events, 32.3 us)
Async XLA Ops:
  7.2 180.6 %all-reduce.2.cloned.1.call-start = ((), (), s32[]{:S(2)}) async-start(), calls=%async_computation | async-start | bytes 1048576 | tf_op jit(solution)/shard_map/psum | solution.py:41
  9.1 23.8 %collective-permute-start.1 = (f32[5,2,1,64,128]{4,3,2,1,0:T(8,128)}, f32[5,2,1,64,128]{4,3,2,1,0:T(8,128)}, u32[]{:S(2)}, u32[]{:S(2)}) collective-permute-start(f32[5,2,1,64,128]{4,3,2,1,0:T(8,128)} %get-tuple-element.70), channel_id=1, source_target_pairs={{1,0},{2,1},{3,2},{0,3},{5,4},{6,5},{7,6},{4,7},{9,8},{10,9},{11,1... | collective-permute-start | bytes 983048 | tf_op jit(solution)/shard_map/ppermute | solution.py:26
  11.5 21.4 %collective-permute-start.2 = (f32[5,2,1,64,128]{4,3,2,1,0:T(8,128)S(1)}, f32[5,2,1,64,128]{4,3,2,1,0:T(8,128)}, u32[]{:S(2)}, u32[]{:S(2)}) collective-permute-start(f32[5,2,1,64,128]{4,3,2,1,0:T(8,128)S(1)} %get-tuple-element.71), channel_id=1, source_target_pairs={{0,1},{1,2},{2,3},{3,0},{4,5},{5,6},{6,7},{7,4},{8,9},{9,10},{10,1... | collective-permute-start | bytes 983048 | tf_op jit(solution)/shard_map/ppermute | solution.py:24
  13.4 10.2 %copy-start = (f32[1,5,2,8,64,128]{5,4,3,2,1,0:T(8,128)S(1)}, f32[1,5,2,8,64,128]{5,4,3,2,1,0:T(8,128)}, u32[]{:S(2)}) copy-start(f32[1,5,2,8,64,128]{5,4,3,2,1,0:T(8,128)} %param.24) | copy-start | bytes 7864324
  13.4 27.5 %collective-permute-start = (f32[2,8,64,128]{3,2,1,0:T(8,128)}, f32[2,8,64,128]{3,2,1,0:T(8,128)}, u32[]{:S(2)}, u32[]{:S(2)}) collective-permute-start(f32[2,8,64,128]{3,2,1,0:T(8,128)} %slice_bitcast_fusion.3), channel_id=1, source_target_pairs={{0,4},{4,8},{8,12},{12,16},{16,20},{20,24},{24,28},{1,5},{5,9},{9,... | collective-permute-start | bytes 1572872 | tf_op jit(solution)/shard_map/ppermute | solution.py:36
  27.1 3.0 %copy-start.5 = (f32[5]{0:T(128)S(1)}, f32[5]{0:T(128)}, u32[]{:S(2)}) copy-start(f32[5]{0:T(128)} %constant.15.clone) | copy-start | bytes 64
  27.1 3.6 %copy-start.6 = (f32[5]{0:T(128)S(1)}, f32[5]{0:T(128)}, u32[]{:S(2)}) copy-start(f32[5]{0:T(128)} %constant.42.clone) | copy-start | bytes 64
  27.1 4.2 %copy-start.7 = (f32[5]{0:T(128)S(1)}, f32[5]{0:T(128)}, u32[]{:S(2)}) copy-start(f32[5]{0:T(128)} %constant.43.clone) | copy-start | bytes 64
  27.1 4.8 %copy-start.2 = (f32[8,64,128]{2,1,0:T(8,128)S(1)}, f32[8,64,128]{2,1,0:T(8,128)}, u32[]{:S(2)}) copy-start(f32[8,64,128]{2,1,0:T(8,128)} %param.25) | copy-start | bytes 786436
  40.7 0.7 copy-start.3
  40.7 0.7 copy-start.4
  45.3 9.6 %collective-permute-start.4 = (f32[5,2,1,64,128]{4,3,2,1,0:T(8,128)S(1)}, f32[5,2,1,64,128]{4,3,2,1,0:T(8,128)S(1)}, u32[]{:S(2)}, u32[]{:S(2)}) collective-permute-start(f32[5,2,1,64,128]{4,3,2,1,0:T(8,128)S(1)} %get-tuple-element.55), channel_id=1, source_target_pairs={{1,0},{2,1},{3,2},{0,3},{5,4},{6,5},{7,6},{4,7},{9,8},{10,9},{11,1... | collective-permute-start | bytes 983048 | tf_op jit(solution)/shard_map/ppermute | solution.py:26
  46.9 9.1 %collective-permute-start.5 = (f32[5,2,1,64,128]{4,3,2,1,0:T(8,128)S(1)}, f32[5,2,1,64,128]{4,3,2,1,0:T(8,128)S(1)}, u32[]{:S(2)}, u32[]{:S(2)}) collective-permute-start(f32[5,2,1,64,128]{4,3,2,1,0:T(8,128)S(1)} %get-tuple-element.56), channel_id=1, source_target_pairs={{0,1},{1,2},{2,3},{3,0},{4,5},{5,6},{6,7},{7,4},{8,9},{9,10},{10,1... | collective-permute-start | bytes 983048 | tf_op jit(solution)/shard_map/ppermute | solution.py:24
  46.9 15.4 %collective-permute-start.3 = (f32[2,8,64,128]{3,2,1,0:T(8,128)S(1)}, f32[2,8,64,128]{3,2,1,0:T(8,128)}, u32[]{:S(2)}, u32[]{:S(2)}) collective-permute-start(f32[2,8,64,128]{3,2,1,0:T(8,128)S(1)} %slice_bitcast_fusion.2), channel_id=1, source_target_pairs={{0,4},{4,8},{8,12},{12,16},{16,20},{20,24},{24,28},{1,5},{5,9},{9,... | collective-permute-start | bytes 1572872 | tf_op jit(solution)/shard_map/ppermute | solution.py:36
  66.4 8.4 %collective-permute-start.7 = (f32[5,2,1,64,128]{4,3,2,1,0:T(8,128)S(1)}, f32[5,2,1,64,128]{4,3,2,1,0:T(8,128)S(1)}, u32[]{:S(2)}, u32[]{:S(2)}) collective-permute-start(f32[5,2,1,64,128]{4,3,2,1,0:T(8,128)S(1)} %get-tuple-element.40), channel_id=1, source_target_pairs={{1,0},{2,1},{3,2},{0,3},{5,4},{6,5},{7,6},{4,7},{9,8},{10,9},{11,1... | collective-permute-start | bytes 983048 | tf_op jit(solution)/shard_map/ppermute | solution.py:26
  67.0 9.4 %collective-permute-start.8 = (f32[5,2,1,64,128]{4,3,2,1,0:T(8,128)S(1)}, f32[5,2,1,64,128]{4,3,2,1,0:T(8,128)S(1)}, u32[]{:S(2)}, u32[]{:S(2)}) collective-permute-start(f32[5,2,1,64,128]{4,3,2,1,0:T(8,128)S(1)} %get-tuple-element.41), channel_id=1, source_target_pairs={{0,1},{1,2},{2,3},{3,0},{4,5},{5,6},{6,7},{7,4},{8,9},{9,10},{10,1... | collective-permute-start | bytes 983048 | tf_op jit(solution)/shard_map/ppermute | solution.py:24
  67.1 17.7 %collective-permute-start.6 = (f32[2,8,64,128]{3,2,1,0:T(8,128)S(1)}, f32[2,8,64,128]{3,2,1,0:T(8,128)}, u32[]{:S(2)}, u32[]{:S(2)}) collective-permute-start(f32[2,8,64,128]{3,2,1,0:T(8,128)S(1)} %slice_bitcast_fusion.1), channel_id=1, source_target_pairs={{0,4},{4,8},{8,12},{12,16},{16,20},{20,24},{24,28},{1,5},{5,9},{9,... | collective-permute-start | bytes 1572872 | tf_op jit(solution)/shard_map/ppermute | solution.py:36
  88.9 8.3 %collective-permute-start.10 = (f32[5,2,1,64,128]{4,3,2,1,0:T(8,128)S(1)}, f32[5,2,1,64,128]{4,3,2,1,0:T(8,128)S(1)}, u32[]{:S(2)}, u32[]{:S(2)}) collective-permute-start(f32[5,2,1,64,128]{4,3,2,1,0:T(8,128)S(1)} %get-tuple-element.25), channel_id=1, source_target_pairs={{1,0},{2,1},{3,2},{0,3},{5,4},{6,5},{7,6},{4,7},{9,8},{10,9},{11,1... | collective-permute-start | bytes 983048 | tf_op jit(solution)/shard_map/ppermute | solution.py:26
  89.7 9.7 %collective-permute-start.11 = (f32[5,2,1,64,128]{4,3,2,1,0:T(8,128)S(1)}, f32[5,2,1,64,128]{4,3,2,1,0:T(8,128)S(1)}, u32[]{:S(2)}, u32[]{:S(2)}) collective-permute-start(f32[5,2,1,64,128]{4,3,2,1,0:T(8,128)S(1)} %get-tuple-element.26), channel_id=1, source_target_pairs={{0,1},{1,2},{2,3},{3,0},{4,5},{5,6},{6,7},{7,4},{8,9},{9,10},{10,1... | collective-permute-start | bytes 983048 | tf_op jit(solution)/shard_map/ppermute | solution.py:24
  90.5 18.0 %collective-permute-start.9 = (f32[2,8,64,128]{3,2,1,0:T(8,128)}, f32[2,8,64,128]{3,2,1,0:T(8,128)S(1)}, u32[]{:S(2)}, u32[]{:S(2)}) collective-permute-start(f32[2,8,64,128]{3,2,1,0:T(8,128)} %slice_bitcast_fusion), channel_id=1, source_target_pairs={{0,4},{4,8},{8,12},{12,16},{16,20},{20,24},{24,28},{1,5},{5,9},{9,... | collective-permute-start | bytes 1572872 | tf_op jit(solution)/shard_map/ppermute | solution.py:36
  187.8 2.9 %copy-start.1 = (f32[2,8,64,128]{3,2,1,0:T(8,128)S(1)}, f32[2,8,64,128]{3,2,1,0:T(8,128)}, u32[]{:S(2)}) copy-start(f32[2,8,64,128]{3,2,1,0:T(8,128)} %all-reduce.2.cloned.1.call-done) | copy-start | bytes 1572868
  188.7 2.3 %collective-permute-start.12 = (f32[2,1,64,128]{3,2,1,0:T(8,128)S(1)}, f32[2,1,64,128]{3,2,1,0:T(8,128)S(1)}, u32[]{:S(2)}, u32[]{:S(2)}) collective-permute-start(f32[2,1,64,128]{3,2,1,0:T(8,128)S(1)} %get-tuple-element.82), channel_id=1, source_target_pairs={{1,0},{2,1},{3,2},{0,3},{5,4},{6,5},{7,6},{4,7},{9,8},{10,9},{11,1... | collective-permute-start | bytes 196616 | tf_op jit(solution)/shard_map/ppermute | solution.py:26
  188.8 4.4 %collective-permute-start.13 = (f32[2,1,64,128]{3,2,1,0:T(8,128)S(1)}, f32[2,1,64,128]{3,2,1,0:T(8,128)S(1)}, u32[]{:S(2)}, u32[]{:S(2)}) collective-permute-start(f32[2,1,64,128]{3,2,1,0:T(8,128)S(1)} %get-tuple-element.83), channel_id=1, source_target_pairs={{0,1},{1,2},{2,3},{3,0},{4,5},{5,6},{6,7},{7,4},{8,9},{9,10},{10,1... | collective-permute-start | bytes 196616 | tf_op jit(solution)/shard_map/ppermute | solution.py:24
  193.7 0.7 copy-start.8
Sparse Core Ops, SparseCore 0:
  111.8 75.9 all-reduce.1
where the time goes:
time: 204 us; the launch traced here: 203 us
  waiting for transfers between devices  99.7 us (49%)
  local copies, waits for them, and re-layouts  31.2 us (15%)
  other arithmetic  31.1 us (15%)
  starting transfers between devices  26.7 us (13%)
  between operations  14.5 us (7%)
    psum x1, waiting for transfers between devices, from_root(): return lax.psum(jnp.where(mine, x, jnp.zeros_like(x)), axis)  76.1 us
    slice x20, local copies, waits for them, and re-layouts, padded_rates(): total = total + jnp.roll(center, 1, axis_id) + jnp.roll(center, -1, axis_id)  22.9 us
    ppermute x4, starting transfers between devices, passed_along(): return lax.ppermute(block, axis, route)  20.7 us
    add x5, other arithmetic, padded_rates(): total = total + jnp.roll(center, 1, axis_id) + jnp.roll(center, -1, axis_id)  16.3 us
    ppermute x4, waiting for transfers between devices, passed_along(): return lax.ppermute(block, axis, route)  10.5 us
    ppermute x5, waiting for transfers between devices, padded_2(): lax.ppermute(tail, axis, [(i, (i + 1) % count) for i in range(count)])  7.03 us
    ppermute x5, waiting for transfers between devices, padded_2(): lax.ppermute(head, axis, [((i + 1) % count, i) for i in range(count)])  6.02 us
    ppermute x5, starting transfers between devices, padded_2(): lax.ppermute(head, axis, [((i + 1) % count, i) for i in range(count)])  5.44 us
  transfers between devices with their start and end apart: 15, of which 11 were waited for; matrix products, arithmetic and copies ran while one was open for 20% of the time, Pallas kernels for 0%

commit v1 on v0

v1 whole, which is shorter than its diff:
```python
import functools
import math

import jax
import jax.numpy as jnp
import numpy as np
from jax import lax
from jax.experimental import pallas as pl
from jax.experimental.pallas import tpu as pltpu
from jax.sharding import PartitionSpec as P

SWEEPS = 4
LAG = 2

substrate_spread = 0.2
catalyst_spread = 0.1
slab_time = 0.5

MESH = pl.DeviceIdType.MESH


def lobatto_table():
    spread_root = math.sqrt(3.0 / 7.0)
    node_times = [0.0, (1.0 - spread_root) / 2.0, 0.5, (1.0 + spread_root) / 2.0, 1.0]
    table = [[0.0] * 5 for blank in range(5)]
    for column in range(5):
        coeffs = [1.0]
        divisor = 1.0
        for other_node in range(5):
            if other_node != column:
                product = [0.0] * (len(coeffs) + 1)
                for power, entry in enumerate(coeffs):
                    product[power + 1] += entry
                    product[power] -= node_times[other_node] * entry
                coeffs = product
                divisor *= node_times[column] - node_times[other_node]
        for row_index in range(5):
            upper = node_times[row_index]
            total_sum = 0.0
            for power, entry in enumerate(coeffs):
                total_sum += entry / (power + 1) * upper ** (power + 1)
            table[row_index][column] = total_sum / divisor
    return (np.array(node_times), np.array(table))


def rates(below, here, above, feed, drain):
    rows, lanes = here[0].shape

    def lap(i):
        w = here[i]
        around = (pltpu.roll(w, 1, 0) + pltpu.roll(w, rows - 1, 0)) + (
            pltpu.roll(w, 1, 1) + pltpu.roll(w, lanes - 1, 1)
        )
        return around + (below[i] + above[i]) - 6.0 * w

    s, c = here
    reacting = s * c * c
    grow_sub = substrate_spread * lap(0) - reacting + feed * (1.0 - s)
    grow_cat = catalyst_spread * lap(1) + reacting - drain * c
    return grow_sub, grow_cat


def kernel(
    slabs, blocks, weights,
    guess, feed_in, kill_in,
    end_out, last_out, rate_out,
    u, last, feed, drain, fbuf,
    load_sem, fixed_sem, tm_send, tm_recv, halo_send, halo_recv, cast_send, cast_recv,
):
    layers = guess.shape[2]
    rows = guess.shape[3]
    tm = lax.axis_index("tm")
    sp = lax.axis_index("space")
    left = lax.rem(sp + blocks - 1, blocks)
    right = lax.rem(sp + 1, blocks)
    top = slabs // 2 - 1
    a = tm // 2
    b = tm % 2
    source = tm == slabs - 1
    not_source = tm < slabs - 1
    primary = 1 - b

    def layer_of(c):
        half = c // 2
        odd = c % 2
        return half + odd * (layers - 1 - 2 * half)

    loads = [
        pltpu.make_async_copy(guess, u.at[0, :, :, pl.ds(1, layers)], load_sem.at[0]),
        pltpu.make_async_copy(feed_in, feed, load_sem.at[1]),
        pltpu.make_async_copy(kill_in, drain, load_sem.at[2]),
    ]
    for load in loads:
        load.start()

    def fixed(k):
        return pltpu.make_async_copy(guess.at[0], u.at[k, 0, :, pl.ds(1, layers)], fixed_sem.at[k - 1])

    @pl.when(tm == 0)
    def _():
        for k in range(1, SWEEPS + 1):
            fixed(k).start()

    barrier = pltpu.get_barrier_semaphore()
    for hop in (1, 2, slabs - 2, slabs - 1):
        pl.semaphore_signal(barrier, inc=1, device_id={"tm": lax.rem(tm + hop, slabs)}, device_id_type=MESH)
    for side in (left, right):
        pl.semaphore_signal(barrier, inc=1, device_id={"space": side}, device_id_type=MESH)
    pl.semaphore_wait(barrier, 6)

    def stream(k, c, src):
        return pltpu.make_async_remote_copy(
            src_ref=src,
            dst_ref=u.at[k + 1, 0, :, 1 + layer_of(c)],
            send_sem=tm_send.at[k, c],
            recv_sem=tm_recv.at[k, c],
            device_id={"tm": lax.rem(tm + 1, slabs)},
            device_id_type=MESH,
        )

    def halo(k, side, src):
        return pltpu.make_async_remote_copy(
            src_ref=src,
            dst_ref=u.at[k, :, :, (1 - side) * (layers + 1)],
            send_sem=halo_send.at[k, side],
            recv_sem=halo_recv.at[k, side],
            device_id={"space": left + side * (right - left)},
            device_id_type=MESH,
        )

    def own_edge(k, side):
        return u.at[k, :, :, 1 + side * (layers - 1)]

    halo(0, 0, guess.at[:, :, 0]).start()
    halo(0, 1, guess.at[:, :, layers - 1]).start()

    @pl.when(not_source)
    def _():
        @pl.loop(0, layers)
        def _(c):
            stream(0, c, guess.at[4, :, layer_of(c)]).start()

    for load in loads:
        load.wait()
    drain[...] = drain[...] + feed[...]

    @pl.when(tm == 0)
    def _():
        for k in range(1, SWEEPS + 1):
            fixed(k).wait()

    def arrive(k, c):
        @pl.when(c == 0)
        def _():
            halo(k, 1, own_edge(k, 1)).wait_recv()

        @pl.when(c == 1)
        def _():
            halo(k, 0, own_edge(k, 0)).wait_recv()

    def begin(k, c):
        @pl.when(tm > 0)
        def _():
            stream(k, c, u.at[k, 4, :, 1 + layer_of(c)]).wait_recv()

    def all_rates(k, i):
        f, d = feed[i], drain[i]
        for j in range(5):
            below, here, above = ((u[k, j, 0, i + n], u[k, j, 1, i + n]) for n in range(3))
            fbuf[j, 0], fbuf[j, 1] = rates(below, here, above, f, d)

    def step(k, i, nodes):
        @pl.loop(0, rows // 8)
        def _(r):
            at = pl.ds(pl.multiple_of(r * 8, 8), 8)
            for s in range(2):
                start = u[k + 1, 0, s, 1 + i, at]
                grown = [fbuf[j, s, at] for j in range(5)]
                for m in nodes:
                    total = grown[0] * weights[m][0]
                    for j in range(1, 5):
                        total = total + grown[j] * weights[m][j]
                    u[k + 1, m, s, 1 + i, at] = start + total

    @pl.loop(0, SWEEPS - 1)
    def _(k):
        @pl.loop(0, layers)
        def _(c):
            i = layer_of(c)
            arrive(k, c)
            all_rates(k, i)
            begin(k, c)
            step(k, i, (4, 1, 2, 3))

            @pl.when(not_source)
            def _():
                stream(k + 1, c, u.at[k + 1, 4, :, 1 + i]).start()

            @pl.when(c < 2)
            def _():
                halo(k + 1, c, own_edge(k + 1, c)).start()

    def cast(lane, c, species, target):
        at = last.at[species, 1 + layer_of(c)]
        return pltpu.make_async_remote_copy(
            src_ref=at,
            dst_ref=at,
            send_sem=cast_send.at[lane, c],
            recv_sem=cast_recv.at[species, c],
            device_id={"tm": target},
            device_id_type=MESH,
        )

    down_on = a > 0
    cross_on = (a < top) | source
    cross_species = primary + jnp.where(source, 1, 0)
    extra_on = tm == 2 * (top - 1)

    def down(c):
        return cast(0, c, primary, lax.rem(tm + slabs - 2, slabs))

    def cross(c):
        return cast(1, c, cross_species, tm + 1 - 2 * b)

    def extra(c):
        return cast(2, c, 0, lax.rem(tm + 2, slabs))

    def last_halo(side):
        return pltpu.make_async_remote_copy(
            src_ref=last.at[:, 1 + side * (layers - 1)],
            dst_ref=last.at[:, (1 - side) * (layers + 1)],
            send_sem=halo_send.at[SWEEPS, side],
            recv_sem=halo_recv.at[SWEEPS, side],
            device_id={"space": left + side * (right - left)},
            device_id_type=MESH,
        )

    @pl.loop(0, layers + LAG)
    def _(c):
        @pl.when(c < layers)
        def _():
            i = layer_of(c)
            arrive(SWEEPS - 1, c)
            all_rates(SWEEPS - 1, i)
            begin(SWEEPS - 1, c)
            step(SWEEPS - 1, i, (4,))
            end_out[:, i] = u[SWEEPS, 4, :, 1 + i]

            @pl.when(source)
            def _():
                last[:, 1 + i] = u[SWEEPS, 4, :, 1 + i]

            @pl.when(not_source)
            def _():
                cast(0, c, primary, tm).wait_recv()

            @pl.when(down_on)
            def _():
                down(c).start()

            @pl.when(cross_on)
            def _():
                cross(c).start()

        @pl.when(c >= LAG)
        def _():
            late = c - LAG

            @pl.when(not_source)
            def _():
                cast(0, late, 1 - primary, tm).wait_recv()

            @pl.when(extra_on)
            def _():
                extra(late).start()

            @pl.when(late < 2)
            def _():
                last_halo(late).start()

    last_halo(0).wait_recv()
    last_halo(1).wait_recv()

    @pl.loop(0, layers)
    def _(i):
        below, here, above = ((last[0, i + n], last[1, i + n]) for n in range(3))
        grow = rates(below, here, above, feed[i], drain[i])
        for s in range(2):
            last_out[s, i] = here[s]
            rate_out[s, i] = slab_time * grow[s]

    for k in range(SWEEPS):
        for side in range(2):
            halo(k, side, own_edge(k, side)).wait_send()
    last_halo(0).wait_send()
    last_halo(1).wait_send()

    @pl.loop(0, layers)
    def _(c):
        @pl.when(not_source)
        def _():
            for k in range(SWEEPS):
                stream(k, c, u.at[k, 4, :, 1 + layer_of(c)]).wait_send()

        @pl.when(down_on)
        def _():
            down(c).wait_send()

        @pl.when(cross_on)
        def _():
            cross(c).wait_send()

        @pl.when(extra_on)
        def _():
            extra(c).wait_send()


def shards(slabs, blocks, guess, feed_rate, kill_rate):
    node_times, table = lobatto_table()
    weights = [[float(np.float32(slab_time * w)) for w in row] for row in table]
    _, nodes, species, layers, rows, lanes = guess.shape
    pair = jax.ShapeDtypeStruct((species, layers, rows, lanes), jnp.float32)
    dma = pltpu.SemaphoreType.DMA
    end, last, rate = pl.pallas_call(
        functools.partial(kernel, slabs, blocks, weights),
        out_shape=(pair, pair, pair),
        in_specs=[pl.BlockSpec(memory_space=pl.ANY)] * 3,
        out_specs=(pl.BlockSpec(memory_space=pltpu.VMEM),) * 3,
        scratch_shapes=[
            pltpu.VMEM((SWEEPS + 1, nodes, species, layers + 2, rows, lanes), jnp.float32),
            pltpu.VMEM((species, layers + 2, rows, lanes), jnp.float32),
            pltpu.VMEM((layers, rows, lanes), jnp.float32),
            pltpu.VMEM((layers, rows, lanes), jnp.float32),
            pltpu.VMEM((nodes, species, rows, lanes), jnp.float32),
            dma((3,)),
            dma((SWEEPS,)),
            dma((SWEEPS, layers)),
            dma((SWEEPS, layers)),
            dma((SWEEPS + 1, 2)),
            dma((SWEEPS + 1, 2)),
            dma((3, layers)),
            dma((2, layers)),
        ],
        compiler_params=pltpu.CompilerParams(
            collective_id=0, has_side_effects=True, vmem_limit_bytes=40 * 1024 * 1024
        ),
    )(guess[0], feed_rate, kill_rate)
    offsets = jnp.asarray(node_times, jnp.float32).reshape((-1, 1, 1, 1, 1))
    next_one = last[None] + offsets * rate[None]
    return (end[None], next_one[None])


def solution(mesh):
    placed = (
        P("tm", None, None, "space", None, None),
        P("space", None, None),
        P("space", None, None),
    )
    return jax.shard_map(
        functools.partial(shards, mesh.shape["tm"], mesh.shape["space"]),
        mesh=mesh,
        in_specs=placed,
        out_specs=(P("tm", None, "space", None, None), P("tm", None, None, "space", None, None)),
        check_vma=False,
    )
```

time: 204 us -> 105 us (0.51)
  waiting for transfers between devices: 99.7 us -> 0 us
  Pallas kernels: 0 us -> 97 us
  other arithmetic: 31.1 us -> 1.95 us
  local copies, waits for them, and re-layouts: 31.2 us -> 4.44 us
  starting transfers between devices: 26.7 us -> 0 us
  between operations: 14.5 us -> 0.66 us
    pallas_call x0 -> x1, Pallas kernels: none -> 97 us  [shards(): pl.pallas_call(functools.partial(kernel, slabs, blocks, weights), out_sha...]
    psum x1 -> x0, waiting for transfers between devices: 76.1 us -> none  [from_root(): return lax.psum(jnp.where(mine, x, jnp.zeros_like(x)), axis)]
    slice x28 -> x0, local copies, waits for them, and re-layouts: 27.6 us -> none  [the longest x20 22.9 us: padded_rates(): total = total + jnp.roll(center, 1, axis_id) + jnp.roll(center, -1, axis_id)]
    ppermute x14 -> x0, starting transfers between devices: 26.7 us -> none  [the longest x4 20.7 us: passed_along(): return lax.ppermute(block, axis, route)]
    add x14 -> x1, other arithmetic: 25.6 us -> 1.95 us  [shards(): next_one = last[None] + offsets * rate[None]]
    ppermute x14 -> x0, waiting for transfers between devices: 23.5 us -> none  [the longest x4 10.5 us: passed_along(): return lax.ppermute(block, axis, route)]
    unnamed x18 -> x9, local copies, waits for them, and re-layouts: 0.81 us -> 4.44 us
    select_n x5 -> x0, other arithmetic: 3.36 us -> none  [the longest x1 3.08 us: from_root(): return lax.psum(jnp.where(mine, x, jnp.zeros_like(x)), axis)]
  transfers between devices with their start and end apart: 15 -> 0, of which waited for: 11 -> 0; matrix products, arithmetic and copies ran while one was open for 20% -> 0% of each run, Pallas kernels for 0% -> 0%
where the time goes in v1:
time: 105 us; the launch traced here: 104 us
  Pallas kernels  97 us (92%)
  local copies, waits for them, and re-layouts  4.44 us (4%)
  other arithmetic  1.95 us (2%)
    pallas_call x1, Pallas kernels, shards(): pl.pallas_call(functools.partial(kernel, slabs, blocks, weights), out_sha...  97 us
    unnamed x9, local copies, waits for them, and re-layouts  4.44 us

profile of v1, /device:TPU:0, one launch (start us, length us, event | category | flops | bytes accessed | tf_op | source)
XLA Modules:
  0.0 104.1 jit_solution(1064676290473722943)
XLA Ops:
  0.6 0.0 copy-start.3
  0.6 0.0 copy-start
  0.7 1.7 %copy-done = f32[1,5,2,8,64,128]{5,4,3,2,1,0:T(8,128)S(1)} copy-done((f32[1,5,2,8,64,128]{5,4,3,2,1,0:T(8,128)S(1)}, f32[1,5,2,8,64,128]{5,4,3,2,1,0:T(8,128)}, u32[]{:S(2)}) %copy-start) | copy-done | bytes 2621464
  2.4 0.0 copy-start.1
  2.4 0.9 copy-done.1
  3.3 0.0 copy-start.2
  3.3 0.9 copy-done.2
  4.3 97.0 %shard_map.59 = (f32[2,8,64,128]{3,2,1,0:T(8,128)S(1)}, f32[2,8,64,128]{3,2,1,0:T(8,128)S(1)}, f32[2,8,64,128]{3,2,1,0:T(8,128)S(1)}) custom-call(f32[5,2,8,64,128]{4,3,2,1,0:T(8,128)S(1)} %bitcast.2, f32[8,64,128]{2,1,0:T(8,128)S(1)} %copy-done.1, f32[8,64,128]{2,1,0:T(8,128)S(1)} %copy-done.2), custom_call_target="tpu_custom_call" | custom-call | tf_op jit(solution)/shard_map/pallas_call | solution.py:324
  101.3 0.0 copy-done.3
  101.3 2.0 %multiply_add_fusion = f32[1,5,2,8,64,128]{5,4,3,2,1,0:T(8,128)} fusion(f32[2,8,64,128]{3,2,1,0:T(8,128)S(1)} %get-tuple-element.7, f32[5]{0:T(128)S(1)} %copy-done.3, f32[2,8,64,128]{3,2,1,0:T(8,128)S(1)} %get-tuple-element.6), kind=kLoop, calls=%fused_computation | loop fusion | flops 1310720 | bytes 3670036 | tf_op jit(solution)/shard_map/add | solution.py:349
  103.3 0.8 copy.7
Async XLA Ops:
  0.6 100.7 %copy-start.3 = (f32[5]{0:T(128)S(1)}, f32[5]{0:T(128)}, u32[]{:S(2)}) copy-start(f32[5]{0:T(128)} %constant.2.clone) | copy-start | bytes 64
  0.6 1.7 %copy-start = (f32[1,5,2,8,64,128]{5,4,3,2,1,0:T(8,128)S(1)}, f32[1,5,2,8,64,128]{5,4,3,2,1,0:T(8,128)}, u32[]{:S(2)}) copy-start(f32[1,5,2,8,64,128]{5,4,3,2,1,0:T(8,128)} %param.4) | copy-start | bytes 7864324
  2.4 0.9 copy-start.1
  3.3 0.9 copy-start.2

commit v2 on v1

--- a/solution.py
+++ b/solution.py
@@ -262,22 +262,23 @@
             def _():
                 cross(c).start()
 
-        @pl.when(c >= LAG)
+        @pl.when((c >= LAG) & extra_on)
         def _():
             late = c - LAG
-
-            @pl.when(not_source)
-            def _():
-                cast(0, late, 1 - primary, tm).wait_recv()
-
-            @pl.when(extra_on)
-            def _():
-                extra(late).start()
-
-            @pl.when(late < 2)
-            def _():
-                last_halo(late).start()
-
+            cast(0, late, 1 - primary, tm).wait_recv()
+            extra(late).start()
+
+    def rest(first, stop):
+        @pl.when(not_source & (tm != 2 * (top - 1)))
+        def _():
+            @pl.loop(first, stop)
+            def _(c):
+                cast(0, c, 1 - primary, tm).wait_recv()
+
+    rest(0, 2)
+    last_halo(0).start()
+    last_halo(1).start()
+    rest(2, layers)
     last_halo(0).wait_recv()
     last_halo(1).wait_recv()
 
@@ -324,7 +325,7 @@
     end, last, rate = pl.pallas_call(
         functools.partial(kernel, slabs, blocks, weights),
         out_shape=(pair, pair, pair),
-        in_specs=[pl.BlockSpec(memory_space=pl.ANY)] * 3,
+        in_specs=[pl.BlockSpec(memory_space=pltpu.HBM)] * 3,
         out_specs=(pl.BlockSpec(memory_space=pltpu.VMEM),) * 3,
         scratch_shapes=[
             pltpu.VMEM((SWEEPS + 1, nodes, species, layers + 2, rows, lanes), jnp.float32),

time: 105 us -> 78.7 us (0.75)
  Pallas kernels: 97 us -> 70.1 us
    pallas_call x1, Pallas kernels: 97 us -> 70.1 us  [shards(): pl.pallas_call(functools.partial(kernel, slabs, blocks, weights), out_sha...]
where the time goes in v2:
time: 78.7 us; the launch traced here: 77.2 us
  Pallas kernels  70.1 us (89%)
  local copies, waits for them, and re-layouts  4.44 us (6%)
  other arithmetic  1.95 us (2%)
    pallas_call x1, Pallas kernels, shards(): pl.pallas_call(functools.partial(kernel, slabs, blocks, weights), out_sha...  70.1 us
    unnamed x9, local copies, waits for them, and re-layouts  4.44 us
    add x1, other arithmetic, shards(): next_one = last[None] + offsets * rate[None]  1.95 us

profile of v2, /device:TPU:0, one launch (start us, length us, event | category | flops | bytes accessed | tf_op | source)
XLA Modules:
  0.0 77.2 jit_solution(16008850762547782299)
XLA Ops:
  0.6 0.0 copy-start.3
  0.6 0.0 copy-start
  0.7 1.7 %copy-done = f32[1,5,2,8,64,128]{5,4,3,2,1,0:T(8,128)S(1)} copy-done((f32[1,5,2,8,64,128]{5,4,3,2,1,0:T(8,128)S(1)}, f32[1,5,2,8,64,128]{5,4,3,2,1,0:T(8,128)}, u32[]{:S(2)}) %copy-start) | copy-done | bytes 2621464
  2.4 0.0 copy-start.1
  2.4 0.9 %copy-done.1 = f32[8,64,128]{2,1,0:T(8,128)S(1)} copy-done((f32[8,64,128]{2,1,0:T(8,128)S(1)}, f32[8,64,128]{2,1,0:T(8,128)}, u32[]{:S(2)}) %copy-start.1) | copy-done | bytes 262168
  3.3 0.0 copy-start.2
  3.3 0.9 %copy-done.2 = f32[8,64,128]{2,1,0:T(8,128)S(1)} copy-done((f32[8,64,128]{2,1,0:T(8,128)S(1)}, f32[8,64,128]{2,1,0:T(8,128)}, u32[]{:S(2)}) %copy-start.2) | copy-done | bytes 262168
  4.3 70.1 %shard_map.59 = (f32[2,8,64,128]{3,2,1,0:T(8,128)S(1)}, f32[2,8,64,128]{3,2,1,0:T(8,128)S(1)}, f32[2,8,64,128]{3,2,1,0:T(8,128)S(1)}) custom-call(f32[5,2,8,64,128]{4,3,2,1,0:T(8,128)S(1)} %bitcast.2, f32[8,64,128]{2,1,0:T(8,128)S(1)} %copy-done.1, f32[8,64,128]{2,1,0:T(8,128)S(1)} %copy-done.2), custom_call_target="tpu_custom_call" | custom-call | tf_op jit(solution)/shard_map/pallas_call | solution.py:325
  74.4 0.0 copy-done.3
  74.5 2.0 %multiply_add_fusion = f32[1,5,2,8,64,128]{5,4,3,2,1,0:T(8,128)} fusion(f32[2,8,64,128]{3,2,1,0:T(8,128)S(1)} %get-tuple-element.7, f32[5]{0:T(128)S(1)} %copy-done.3, f32[2,8,64,128]{3,2,1,0:T(8,128)S(1)} %get-tuple-element.6), kind=kLoop, calls=%fused_computation | loop fusion | flops 1310720 | bytes 3670036 | tf_op jit(solution)/shard_map/add | solution.py:350
  76.4 0.8 %copy.7 = f32[1,2,8,64,128]{4,3,2,1,0:T(8,128)} copy(f32[1,2,8,64,128]{4,3,2,1,0:T(8,128)S(1)} %bitcast.3) | data formatting | bytes 1048576
Async XLA Ops:
  0.6 73.8 %copy-start.3 = (f32[5]{0:T(128)S(1)}, f32[5]{0:T(128)}, u32[]{:S(2)}) copy-start(f32[5]{0:T(128)} %constant.2.clone) | copy-start | bytes 64
  0.6 1.7 %copy-start = (f32[1,5,2,8,64,128]{5,4,3,2,1,0:T(8,128)S(1)}, f32[1,5,2,8,64,128]{5,4,3,2,1,0:T(8,128)}, u32[]{:S(2)}) copy-start(f32[1,5,2,8,64,128]{5,4,3,2,1,0:T(8,128)} %param.4) | copy-start | bytes 7864324
  2.4 0.9 %copy-start.1 = (f32[8,64,128]{2,1,0:T(8,128)S(1)}, f32[8,64,128]{2,1,0:T(8,128)}, u32[]{:S(2)}) copy-start(f32[8,64,128]{2,1,0:T(8,128)} %feed_in.1) | copy-start | bytes 786436
  3.3 0.9 %copy-start.2 = (f32[8,64,128]{2,1,0:T(8,128)S(1)}, f32[8,64,128]{2,1,0:T(8,128)}, u32[]{:S(2)}) copy-start(f32[8,64,128]{2,1,0:T(8,128)} %kill_in.1) | copy-start | bytes 786436
